TPU v7x, 32 devices: a whole 2x2x4 slice. The times are simulated.
32 devices in a mesh: freq: 4 (over y, x), tile: 8 (over z, core).
Axes of the slice: x: 2, y: 2, z: 4, core: 2. Of those that a mesh axis runs over, the one named last changes fastest.
Arguments:
- voltages: bfloat16 [4096, 24960], P(('freq', 'tile')), may hold values from -16 to 16, as said below
- channel_ids: int32 [12], replicated, may hold values from 1 to 63
- start_basis: float32 [2, 8, 4096], replicated, may hold values from -0.0625 to 0.0625
Outputs:
- cleaned: float32 [2, 12, 192, 4096], P(None, 'freq', 'tile')
Inputs may be any that keep to these rules, and one draw needn't show every extreme that they name: `voltages`: real samples of each input over the whole window.
All inputs are finite; a program needn't handle non-finite values.
Results may differ from a plain program's by a relative error of at most 0.0048.
Values may be sent and summed in bfloat16 or wider, within the bound.
A program may use at most 128 MiB of HBM per device.

v0:
```python
import functools
import math

import jax
import jax.numpy as jnp
from jax import lax
from jax.experimental import pallas as pl
from jax.experimental.pallas import tpu as pltpu
from jax.sharding import PartitionSpec as P

TAPS = 4
P_SIZE = 128
ITERS = 3
STEP = 16

loading = 0.5
highest = lax.Precision.HIGHEST
VMEM = pl.BlockSpec(memory_space=pltpu.VMEM)
MESH = pl.DeviceIdType.MESH


def make_table(channel_ids, taps_count, points):
    length = taps_count * points
    offsets = jnp.arange(length, dtype=jnp.float32)
    shifted = (offsets + 0.5 - length / 2.0) / points
    window = jnp.sinc(shifted) * (0.5 - 0.5 * jnp.cos(2.0 * math.pi * (offsets + 0.5) / length))
    window = window / jnp.sqrt(jnp.sum(window * window))
    window = window.reshape(taps_count, points)
    phases = channel_ids[:, None] * jnp.arange(points, dtype=jnp.int32)[None, :] % points
    angles = 2.0 * math.pi / points * phases.astype(jnp.float32)
    rotors = jnp.stack([jnp.cos(angles), -jnp.sin(angles)])
    return (window[:, None, None, :] * rotors[None]).astype(jnp.bfloat16)


def banded(coeffs):
    rows = coeffs.shape[1]
    spect = lax.broadcasted_iota(jnp.int32, (1, STEP, STEP + TAPS - 1, 1), 1)
    frame = lax.broadcasted_iota(jnp.int32, (1, STEP, STEP + TAPS - 1, 1), 2)
    table = jnp.zeros((rows, STEP, STEP + TAPS - 1, P_SIZE), jnp.bfloat16)
    for tap in range(TAPS):
        table = jnp.where(frame - spect == tap, coeffs[tap][:, None, None, :], table)
    return table.reshape(rows * STEP, (STEP + TAPS - 1) * P_SIZE)


def nt(left, right):
    return lax.dot_general(left, right, (((1,), (1,)), ((), ())), preferred_element_type=jnp.float32)


def channelize_kernel(volts_ref, table_ref, out_ref):
    step = pl.program_id(0)
    span = (STEP + TAPS - 1) * P_SIZE
    start = pl.multiple_of(step * (STEP * P_SIZE), P_SIZE)
    chunk = volts_ref[:, pl.ds(start, span)]
    result = nt(table_ref[...], chunk)
    out_ref[...] = result.reshape(out_ref.shape).astype(jnp.bfloat16)


def channelize(voltages, table, rows, spectra_all):
    inputs_local, samples = voltages.shape
    return pl.pallas_call(
        channelize_kernel,
        grid=(spectra_all // STEP,),
        in_specs=[VMEM, VMEM],
        out_specs=pl.BlockSpec((rows, STEP, inputs_local), lambda i: (0, i, 0)),
        out_shape=jax.ShapeDtypeStruct((rows, spectra_all, inputs_local), jnp.bfloat16),
        compiler_params=pltpu.CompilerParams(vmem_limit_bytes=40 * 2**20),
    )(voltages, table)


def split3(value):
    high = value.astype(jnp.bfloat16)
    rest = value - high.astype(jnp.float32)
    mid = rest.astype(jnp.bfloat16)
    low = (rest - mid.astype(jnp.float32)).astype(jnp.bfloat16)
    return jnp.concatenate([high, mid, low], axis=0)


def fold3(value):
    rows = value.shape[0] // 3
    return value[:rows] + value[rows : 2 * rows] + value[2 * rows :]


def plain(left, right):
    return lax.dot_general(left, right, (((1,), (0,)), ((), ())), preferred_element_type=jnp.float32)


def project(z, real_v, imag_v, k):
    parts = split3(z)
    on_re = fold3(nt(parts, real_v))
    on_im = fold3(nt(parts, imag_v))
    return jnp.concatenate([on_re[:k] + on_im[k:], on_re[k:] - on_im[:k]], axis=0)


def inverse_factor(gram, k):
    lanes = gram.shape[1]
    col = lax.broadcasted_iota(jnp.int32, (k, lanes), 1)
    row = lax.broadcasted_iota(jnp.int32, (k, lanes), 0)
    zero = jnp.zeros((k, lanes), jnp.float32)
    a_re = gram[:k]
    a_im = gram[k:]
    m_re = jnp.where(col == row, 1.0, zero)
    m_im = zero
    for j in range(k):
        at_col = col == j
        c_re = jnp.sum(jnp.where(at_col, a_re, 0.0), axis=1, keepdims=True)
        c_im = jnp.sum(jnp.where(at_col, a_im, 0.0), axis=1, keepdims=True)
        pivot = jnp.sqrt(c_re[j : j + 1])
        l_re = jnp.where(row[:, :1] > j, c_re / pivot, 0.0)
        l_im = jnp.where(row[:, :1] > j, c_im / pivot, 0.0)
        ar, ai = a_re[j : j + 1] / pivot, a_im[j : j + 1] / pivot
        mr, mi = m_re[j : j + 1] / pivot, m_im[j : j + 1] / pivot
        here = row == j
        a_re = jnp.where(here, ar, a_re - (l_re * ar - l_im * ai))
        a_im = jnp.where(here, ai, a_im - (l_re * ai + l_im * ar))
        m_re = jnp.where(here, mr, m_re - (l_re * mr - l_im * mi))
        m_im = jnp.where(here, mi, m_im - (l_re * mi + l_im * mr))
    return m_re, -m_im


def mix(m_re, m_im, rows, k):
    out_re = jnp.zeros((k, rows.shape[1]), jnp.float32)
    out_im = jnp.zeros((k, rows.shape[1]), jnp.float32)
    for j in range(k):
        f_re, f_im = m_re[:, j : j + 1], m_im[:, j : j + 1]
        r_re, r_im = rows[j : j + 1], rows[k + j : k + j + 1]
        out_re = out_re + (f_re * r_re - f_im * r_im)
        out_im = out_im + (f_re * r_im + f_im * r_re)
    return jnp.concatenate([out_re, out_im], axis=0)


def start_kernel(v_ref, q_ref, pg_ref, *, k, lanes):
    chans, _, spectra, _ = v_ref.shape
    pg_ref[...] = jnp.zeros_like(pg_ref)
    for c in range(chans):
        pg_ref[2 * k * c : 2 * k * (c + 1), :spectra] = project(q_ref[...], v_ref[c, 0], v_ref[c, 1], k)


def step_kernel(v_ref, z_ref, pg_ref, z_out, pg_out, *, k, lanes, first):
    chans, _, spectra, width = v_ref.shape
    pg_out[...] = jnp.zeros_like(pg_out)
    for c in range(chans):
        at = slice(2 * k * c, 2 * k * (c + 1))
        weights = pg_ref[at, :spectra]
        basis = z_ref[...] if first else z_ref[c]
        if not first:
            m_re, m_im = inverse_factor(pg_ref[at, lanes:], k)
            weights = mix(m_re, m_im, weights, k)
            basis = mix(m_re, m_im, basis, k)
        real_v, imag_v = v_ref[c, 0], v_ref[c, 1]
        parts = split3(weights / spectra)
        on_re = fold3(plain(parts, real_v))
        on_im = fold3(plain(parts, imag_v))
        z = jnp.concatenate([on_re[:k] - on_im[k:], on_re[k:] + on_im[:k]], axis=0) + loading * basis
        z_out[c] = z
        pg_out[at, :spectra] = project(z, real_v, imag_v, k)
        pad = jnp.zeros((lanes_pad(k), width), jnp.float32)
        right = jnp.concatenate([z[:k], pad], axis=0)
        right_im = jnp.concatenate([z[k:], pad], axis=0)
        dims = (((1,), (1,)), ((), ()))
        first_dot = lax.dot_general(z, right, dims, precision=highest, preferred_element_type=jnp.float32)
        second_dot = lax.dot_general(z, right_im, dims, precision=highest, preferred_element_type=jnp.float32)
        g_re = first_dot[:k] + second_dot[k:]
        g_im = second_dot[:k] - first_dot[k:]
        pg_out[at, lanes:] = jnp.concatenate([g_re, g_im], axis=0)


def lanes_pad(k):
    return 128 - k


def tn(left, right):
    return lax.dot_general(left, right, (((0,), (0,)), ((), ())), preferred_element_type=jnp.float32)


def clean_kernel(v_ref, z_ref, pg_ref, out_ref, *, k, lanes):
    chans, _, spectra, width = v_ref.shape
    parts_count, _, _, block, _ = out_ref.shape
    for c in range(chans):
        at = slice(2 * k * c, 2 * k * (c + 1))
        m_re, m_im = inverse_factor(pg_ref[at, lanes:], k)
        w = mix(m_re, m_im, pg_ref[at, :spectra], k)
        q = mix(m_re, m_im, z_ref[c], k)
        turned = jnp.concatenate([q[k:], -q[:k]], axis=0)
        w3 = split3(w)
        n2 = 2 * k
        w_left = jnp.concatenate([w3[:n2], w3[:n2], w3[n2 : 2 * n2], w3[n2 : 2 * n2], w3[:n2], w3[2 * n2 :]], axis=0)
        for r, side in ((0, q), (1, turned)):
            s3 = split3(side)
            s_right = jnp.concatenate(
                [s3[:n2], s3[n2 : 2 * n2], s3[:n2], s3[n2 : 2 * n2], s3[2 * n2 :], s3[:n2]], axis=0
            )
            fitted = tn(w_left, s_right)
            cleaned = v_ref[c, r].astype(jnp.float32) - fitted
            out_ref[:, r, c] = cleaned.reshape(parts_count, block, width).astype(jnp.bfloat16)


def reduce_kernel(x_ref, out_ref, land_ref, send1, recv1, send2, recv2, *, size, chunk):
    me = lax.axis_index("tile")
    barrier = pltpu.get_barrier_semaphore()
    for d in range(1, size):
        peer = lax.rem(me + d, size)
        pl.semaphore_signal(barrier, inc=1, device_id={"tile": peer}, device_id_type=MESH)
    pl.semaphore_wait(barrier, size - 1)
    mine = pl.ds(pl.multiple_of(me * chunk, 8), chunk)
    sends = []
    for d in range(1, size):
        peer = lax.rem(me + d, size)
        copy = pltpu.make_async_remote_copy(
            src_ref=x_ref.at[pl.ds(pl.multiple_of(peer * chunk, 8), chunk)],
            dst_ref=land_ref.at[d - 1],
            send_sem=send1.at[d - 1],
            recv_sem=recv1.at[d - 1],
            device_id={"tile": peer},
            device_id_type=MESH,
        )
        copy.start()
        sends.append(copy)
    total = x_ref[mine]
    for d in range(1, size):
        sends[d - 1].wait_recv()
        total = total + land_ref[d - 1]
    out_ref[mine] = total
    later = []
    for d in range(1, size):
        peer = lax.rem(me + d, size)
        copy = pltpu.make_async_remote_copy(
            src_ref=out_ref.at[mine],
            dst_ref=out_ref.at[mine],
            send_sem=send2.at[d - 1],
            recv_sem=recv2.at[d - 1],
            device_id={"tile": peer},
            device_id_type=MESH,
        )
        copy.start()
        later.append(copy)
    for copy in later:
        copy.wait_recv()
    for copy in sends + later:
        copy.wait_send()


def tile_sum(x, size):
    rows, width = x.shape
    chunk = rows // size
    return pl.pallas_call(
        functools.partial(reduce_kernel, size=size, chunk=chunk),
        in_specs=[VMEM],
        out_specs=VMEM,
        out_shape=jax.ShapeDtypeStruct(x.shape, jnp.float32),
        scratch_shapes=[pltpu.VMEM((size - 1, chunk, width), jnp.float32)]
        + [pltpu.SemaphoreType.DMA((size - 1,))] * 4,
        compiler_params=pltpu.CompilerParams(collective_id=0, has_side_effects=True),
    )(x)


def up(value, unit):
    return -(-value // unit) * unit


def body(voltages, channel_ids, start_basis):
    inputs_local, samples_count = voltages.shape
    freq_count = lax.axis_size("freq")
    tile_count = lax.axis_size("tile")
    channels = channel_ids.shape[0]
    chan_local = channels // freq_count
    spectra_all = samples_count // P_SIZE - TAPS + 1
    spectra_local = spectra_all // tile_count
    k = start_basis.shape[1]
    width = freq_count * inputs_local

    coeffs = make_table(channel_ids, TAPS, P_SIZE).reshape(TAPS, 2 * channels, P_SIZE)
    local = channelize(voltages, banded(coeffs), 2 * channels, spectra_all)
    parcel = local.reshape(2, freq_count, chan_local, spectra_all, inputs_local)
    arrived = lax.all_to_all(parcel, "freq", split_axis=1, concat_axis=1, tiled=True)
    values = jnp.transpose(arrived, (2, 0, 3, 1, 4)).reshape(chan_local, 2, spectra_all, width)

    mine = lax.axis_index("tile")
    start = start_basis.reshape(2 * k, freq_count, tile_count, inputs_local)
    start = lax.dynamic_index_in_dim(start, mine, 2, keepdims=False).reshape(2 * k, width)

    lanes = up(spectra_all, 128)
    chunk = up(-(-chan_local * 2 * k // tile_count), 8)
    packed = jax.ShapeDtypeStruct((tile_count * chunk, lanes + 128), jnp.float32)
    z_shape = jax.ShapeDtypeStruct((chan_local, 2 * k, width), jnp.float32)
    params = pltpu.CompilerParams(vmem_limit_bytes=40 * 2**20)

    partial = pl.pallas_call(
        functools.partial(start_kernel, k=k, lanes=lanes),
        in_specs=[VMEM] * 2, out_specs=VMEM, out_shape=packed, compiler_params=params,
    )(values, start)
    z = start
    for step_at in range(ITERS):
        total = tile_sum(partial, tile_count)
        z, partial = pl.pallas_call(
            functools.partial(step_kernel, k=k, lanes=lanes, first=step_at == 0),
            in_specs=[VMEM] * 3, out_specs=[VMEM] * 2, out_shape=[z_shape, packed],
            compiler_params=params,
        )(values, z, total)
    total = tile_sum(partial, tile_count)
    cleaned = pl.pallas_call(
        functools.partial(clean_kernel, k=k, lanes=lanes),
        in_specs=[VMEM] * 3, out_specs=VMEM,
        out_shape=jax.ShapeDtypeStruct((tile_count, 2, chan_local, spectra_local, width), jnp.bfloat16),
        compiler_params=params,
    )(values, z, total)
    moved = lax.all_to_all(cleaned, "tile", split_axis=0, concat_axis=0, tiled=True)
    moved = moved.reshape(tile_count, 2, chan_local, spectra_local, freq_count, inputs_local)
    moved = jnp.transpose(moved, (1, 2, 3, 4, 0, 5)).astype(jnp.float32)
    return moved.reshape(2, chan_local, spectra_local, freq_count * tile_count * inputs_local)


def solution(mesh):
    in_specs = (P(("freq", "tile"), None), P(), P())
    out_specs = P(None, "freq", "tile", None)
    return jax.shard_map(body, mesh=mesh, in_specs=in_specs, out_specs=out_specs, check_vma=False)
```

profile of v0, /device:TPU:1, one launch (start us, length us, event | category | flops | bytes accessed | tf_op | source)
XLA Modules:
  0.0 136.8 jit_solution(14095251535910748280)
XLA Ops:
  0.0 0.7 fusion.44
  1.4 0.1 fusion.20
  1.4 0.8 fusion.10
  2.3 0.0 copy-start
  2.3 0.9 select_select_fusion
  3.2 0.3 copy.22
  3.5 1.7 %copy-done = bf16[128,24960]{1,0:T(8,128)(2,1)S(1)} copy-done((bf16[128,24960]{1,0:T(8,128)(2,1)S(1)}, bf16[128,24960]{1,0:T(8,128)(2,1)}, u32[]{:S(2)}) %copy-start) | copy-done | bytes 6389784
  5.1 8.3 %shard_map.37 = bf16[24,192,128]{2,1,0:T(8,128)(2,1)S(1)} custom-call(bf16[128,24960]{1,0:T(8,128)(2,1)S(1)} %copy-done, bf16[384,2432]{1,0:T(8,128)(2,1)S(1)} %bitcast.28), custom_call_target="tpu_custom_call" | custom-call | tf_op jit(solution)/shard_map/pallas_call | solution.py:60
  13.4 0.0 copy-start.9
  13.4 1.1 copy.10
  14.5 4.3 %all-to-all-start = ((bf16[2,4,3,192,128]{4,3,0,2,1:T(8,128)(2,1)}), bf16[2,4,3,192,128]{4,3,0,2,1:T(8,128)(2,1)S(1)}, u32[]{:S(2)}, u32[]{:S(2)}) async-start(bf16[2,4,3,192,128]{4,3,0,2,1:T(8,128)(2,1)} %copy.10), calls=%async_computation | async-start | bytes 2359296 | tf_op jit(solution)/shard_map/all_to_all | solution.py:274
  18.8 0.0 copy-done.9
  18.8 0.1 copy.17
  18.9 14.4 %all-to-all-done = bf16[2,4,3,192,128]{4,3,0,2,1:T(8,128)(2,1)S(1)} async-done(((bf16[2,4,3,192,128]{4,3,0,2,1:T(8,128)(2,1)}), bf16[2,4,3,192,128]{4,3,0,2,1:T(8,128)(2,1)S(1)}, u32[]{:S(2)}, u32[]{:S(2)}) %all-to-all-start) | async-done | bytes 1179680 | tf_op jit(solution)/shard_map/all_to_all | solution.py:274
  33.3 0.1 copy_bitcast_fusion.1.v_ref
  33.5 0.4 shard_map.38.x_ref
  33.9 0.0 copy-start.3
  33.9 0.7 copy-done.3
  34.6 14.6 %shard_map.39.pg_ref = f32[64,384]{1,0:T(8,128)} custom-call(f32[64,384]{1,0:T(8,128)} %copy-done.3), custom_call_target="tpu_custom_call" | custom-call | tf_op jit(solution)/shard_map/pallas_call | solution.py:245
  49.1 0.0 copy-start.2
  49.2 0.9 copy-done.2
  50.0 1.2 shard_map.40
  51.3 0.0 copy-start.6
  51.3 0.7 copy-done.6
  52.0 11.1 %shard_map.41.pg_ref = f32[64,384]{1,0:T(8,128)} custom-call(f32[64,384]{1,0:T(8,128)} %copy-done.6), custom_call_target="tpu_custom_call" | custom-call | tf_op jit(solution)/shard_map/pallas_call | solution.py:245
  63.0 0.0 copy-start.4
  63.0 0.9 copy-done.4
  63.9 2.5 %shard_map.42 = (f32[3,16,512]{2,1,0:T(8,128)S(1)}, f32[64,384]{1,0:T(8,128)S(1)}) custom-call(bf16[3,2,192,512]{3,2,1,0:T(8,128)(2,1)S(1)} %copy_bitcast_fusion.1.v_ref, f32[3,16,512]{2,1,0:T(8,128)S(1)} %get-tuple-element.11.z_ref, f32[64,384]{1,0:T(8,128)S(1)} %copy-done.4), custom_call_target="tpu_custom_call" | custom-call | tf_op jit(solution)/shard_map/pallas_call | solution.py:294
  66.5 0.0 copy-start.7
  66.5 0.7 copy-done.7
  67.1 12.4 %shard_map.43.pg_ref = f32[64,384]{1,0:T(8,128)} custom-call(f32[64,384]{1,0:T(8,128)} %copy-done.7), custom_call_target="tpu_custom_call" | custom-call | tf_op jit(solution)/shard_map/pallas_call | solution.py:245
  79.6 0.0 copy-start.5
  79.6 0.9 copy-done.5
  80.5 2.5 %shard_map.44 = (f32[3,16,512]{2,1,0:T(8,128)S(1)}, f32[64,384]{1,0:T(8,128)S(1)}) custom-call(bf16[3,2,192,512]{3,2,1,0:T(8,128)(2,1)S(1)} %copy_bitcast_fusion.1.v_ref, f32[3,16,512]{2,1,0:T(8,128)S(1)} %get-tuple-element.13.z_ref, f32[64,384]{1,0:T(8,128)S(1)} %copy-done.5), custom_call_target="tpu_custom_call" | custom-call | tf_op jit(solution)/shard_map/pallas_call | solution.py:294
  83.0 0.0 copy-start.8
  83.0 0.7 copy-done.8
  83.7 11.3 %shard_map.45.pg_ref = f32[64,384]{1,0:T(8,128)} custom-call(f32[64,384]{1,0:T(8,128)} %copy-done.8), custom_call_target="tpu_custom_call" | custom-call | tf_op jit(solution)/shard_map/pallas_call | solution.py:245
  95.0 0.0 copy-start.1
  95.0 0.9 copy-done.1
  95.8 1.6 %shard_map.46 = bf16[8,2,3,24,512]{4,3,2,1,0:T(8,128)(2,1)S(1)} custom-call(bf16[3,2,192,512]{3,2,1,0:T(8,128)(2,1)S(1)} %copy_bitcast_fusion.1.v_ref, f32[3,16,512]{2,1,0:T(8,128)S(1)} %get-tuple-element.15.z_ref, f32[64,384]{1,0:T(8,128)S(1)} %copy-done.1), custom_call_target="tpu_custom_call" | custom-call | tf_op jit(solution)/shard_map/pallas_call | solution.py:300
  97.5 32.4 %all_to_all.10 = bf16[8,2,3,24,512]{4,3,2,1,0:T(8,128)(2,1)S(1)} all-to-all(bf16[8,2,3,24,512]{4,3,2,1,0:T(8,128)(2,1)S(1)} %shard_map.46), channel_id=1, replica_groups=mesh['freq'=4,'tile'=8] {'tile'}, dimensions={0} | all-to-all | bytes 2359296 | tf_op jit(solution)/shard_map/all_to_all | solution.py:306
  129.9 0.8 reshape.227
  130.6 2.8 %copy.13 = f32[2,3,24,4,8,128]{5,4,3,2,1,0:T(8,128)} copy(f32[2,3,24,4,8,128]{5,3,2,1,0,4:T(4,128)S(1)} %bitcast.33) | data formatting | bytes 4718592 | tf_op jit(solution)/shard_map/reshape | solution.py:309
  133.4 3.4 %reshape.224 = f32[2,3,24,4096]{3,2,1,0:T(8,128)} reshape(f32[2,3,24,4,8,128]{5,4,3,2,1,0:T(8,128)} %copy.13) | data formatting | bytes 4718592 | tf_op jit(solution)/shard_map/reshape | solution.py:309
  (11 shorter events, 0.1 us)
Async XLA Ops:
  2.3 2.8 %copy-start = (bf16[128,24960]{1,0:T(8,128)(2,1)S(1)}, bf16[128,24960]{1,0:T(8,128)(2,1)}, u32[]{:S(2)}) copy-start(bf16[128,24960]{1,0:T(8,128)(2,1)} %volts_ref.1) | copy-start | bytes 19169284
  13.4 5.4 %copy-start.9 = (f32[2,8,4096]{2,1,0:T(8,128)S(1)}, f32[2,8,4096]{2,1,0:T(8,128)}, u32[]{:S(2)}) copy-start(f32[2,8,4096]{2,1,0:T(8,128)} %param.5) | copy-start | bytes 786436
  14.5 18.8 %all-to-all-start = ((bf16[2,4,3,192,128]{4,3,0,2,1:T(8,128)(2,1)}), bf16[2,4,3,192,128]{4,3,0,2,1:T(8,128)(2,1)S(1)}, u32[]{:S(2)}, u32[]{:S(2)}) async-start(bf16[2,4,3,192,128]{4,3,0,2,1:T(8,128)(2,1)} %copy.10), calls=%async_computation | async-start | bytes 2359296 | tf_op jit(solution)/shard_map/all_to_all | solution.py:274
  33.9 0.7 copy-start.3
  49.1 0.9 copy-start.2
  51.3 0.7 copy-start.6
  63.0 0.9 copy-start.4
  66.5 0.7 copy-start.7
  79.6 0.9 copy-start.5
  83.0 0.7 copy-start.8
  95.0 0.9 copy-start.1
where the time goes:
time: 138 us; the launch traced here: 137 us
  Pallas kernels  66 us (48%)
  blocking collectives  32.4 us (23%)
  local copies, waits for them, and re-layouts  16.4 us (12%)
  waiting for transfers between devices  14.4 us (10%)
  starting transfers between devices  4.26 us (3%)
  other arithmetic  2.39 us (2%)
    pallas_call x4, Pallas kernels, tile_sum(): pl.pallas_call(functools.partial(reduce_kernel, size=size, chunk=chunk),...  49.4 us
    all_to_all x1, blocking collectives, body(): lax.all_to_all(cleaned, 'tile', split_axis=0, concat_axis=0, tiled=True)  32.4 us
    all_to_all x1, waiting for transfers between devices, body(): lax.all_to_all(parcel, 'freq', split_axis=1, concat_axis=1, tiled=True)  14.4 us
    pallas_call x1, Pallas kernels, channelize(): pl.pallas_call(channelize_kernel, grid=(spectra_all // STEP,), in_specs=[...  8.26 us
    unnamed x23, local copies, waits for them, and re-layouts  8.22 us
    reshape x3, local copies, waits for them, and re-layouts, body(): moved.reshape(2, chan_local, spectra_local, freq_count * tile_count * inp...  6.9 us
    pallas_call x3, Pallas kernels, body(): pl.pallas_call(functools.partial(step_kernel, k=k, lanes=lanes, first=ste...  6.28 us
    all_to_all x1, starting transfers between devices, body(): lax.all_to_all(parcel, 'freq', split_axis=1, concat_axis=1, tiled=True)  4.26 us
  transfers between devices with their start and end apart: 1, of which 1 were waited for; matrix products, arithmetic and copies ran while one was open for 0% of the time, Pallas kernels for 0%

commit v1 on v0

--- a/solution.py
+++ b/solution.py
@@ -46,27 +46,6 @@
     return lax.dot_general(left, right, (((1,), (1,)), ((), ())), preferred_element_type=jnp.float32)
 
 
-def channelize_kernel(volts_ref, table_ref, out_ref):
-    step = pl.program_id(0)
-    span = (STEP + TAPS - 1) * P_SIZE
-    start = pl.multiple_of(step * (STEP * P_SIZE), P_SIZE)
-    chunk = volts_ref[:, pl.ds(start, span)]
-    result = nt(table_ref[...], chunk)
-    out_ref[...] = result.reshape(out_ref.shape).astype(jnp.bfloat16)
-
-
-def channelize(voltages, table, rows, spectra_all):
-    inputs_local, samples = voltages.shape
-    return pl.pallas_call(
-        channelize_kernel,
-        grid=(spectra_all // STEP,),
-        in_specs=[VMEM, VMEM],
-        out_specs=pl.BlockSpec((rows, STEP, inputs_local), lambda i: (0, i, 0)),
-        out_shape=jax.ShapeDtypeStruct((rows, spectra_all, inputs_local), jnp.bfloat16),
-        compiler_params=pltpu.CompilerParams(vmem_limit_bytes=40 * 2**20),
-    )(voltages, table)
-
-
 def split3(value):
     high = value.astype(jnp.bfloat16)
     rest = value - high.astype(jnp.float32)
@@ -91,7 +70,7 @@
     return jnp.concatenate([on_re[:k] + on_im[k:], on_re[k:] - on_im[:k]], axis=0)
 
 
-def inverse_factor(gram, k):
+def inverse_factor(gram, k, off=0):
     lanes = gram.shape[1]
     col = lax.broadcasted_iota(jnp.int32, (k, lanes), 1)
     row = lax.broadcasted_iota(jnp.int32, (k, lanes), 0)
@@ -101,7 +80,7 @@
     m_re = jnp.where(col == row, 1.0, zero)
     m_im = zero
     for j in range(k):
-        at_col = col == j
+        at_col = col == j + off
         c_re = jnp.sum(jnp.where(at_col, a_re, 0.0), axis=1, keepdims=True)
         c_im = jnp.sum(jnp.where(at_col, a_im, 0.0), axis=1, keepdims=True)
         pivot = jnp.sqrt(c_re[j : j + 1])
@@ -126,6 +105,210 @@
         out_re = out_re + (f_re * r_re - f_im * r_im)
         out_im = out_im + (f_re * r_im + f_im * r_re)
     return jnp.concatenate([out_re, out_im], axis=0)
+
+
+def tn(left, right):
+    return lax.dot_general(left, right, (((0,), (0,)), ((), ())), preferred_element_type=jnp.float32)
+
+
+def fused_kernel(
+    volts_ref, table_ref, start_ref, out_ref,
+    stage, v_ref, z_ref, part_ref, land_ref, sum_ref, give_ref,
+    f_send, f_recv, r_send, r_recv, g_send, g_recv, o_send, o_recv, own_sem,
+    *, k, freq, tile, base, off,
+):
+    chans, _, spectra, width = v_ref.shape
+    cols = volts_ref.shape[0]
+    steps = spectra // STEP
+    block = spectra // tile
+    chunk = part_ref.shape[1] // tile
+    group = lax.axis_index("freq")
+    me = lax.axis_index("tile")
+    barrier = pltpu.get_barrier_semaphore()
+    for d in range(1, freq):
+        pl.semaphore_signal(barrier, inc=1, device_id={"freq": lax.rem(group + d, freq)}, device_id_type=MESH)
+    for d in range(1, tile):
+        pl.semaphore_signal(barrier, inc=1, device_id={"tile": lax.rem(me + d, tile)}, device_id_type=MESH)
+    pl.semaphore_wait(barrier, freq - 1 + tile - 1)
+
+    span = (STEP + TAPS - 1) * P_SIZE
+    my_cols = pl.ds(pl.multiple_of(group * cols, cols), cols)
+
+    def handover(i, d):
+        peer = lax.rem(group + d, freq)
+        rows = pl.ds(pl.multiple_of(i * STEP, STEP), STEP)
+        return pltpu.make_async_remote_copy(
+            src_ref=stage.at[peer, :, :, rows, :],
+            dst_ref=v_ref.at[:, :, rows, my_cols],
+            send_sem=f_send.at[i, d - 1],
+            recv_sem=f_recv.at[i, d - 1],
+            device_id={"freq": peer},
+            device_id_type=MESH,
+        )
+
+    def own_part(i):
+        rows = pl.ds(pl.multiple_of(i * STEP, STEP), STEP)
+        return pltpu.make_async_copy(
+            stage.at[group, :, :, rows, :], v_ref.at[:, :, rows, my_cols], own_sem.at[i]
+        )
+
+    def filter_step(i, carry):
+        start = pl.multiple_of(i * (STEP * P_SIZE), P_SIZE)
+        result = nt(table_ref[...], volts_ref[:, pl.ds(start, span)])
+        rows = pl.ds(pl.multiple_of(i * STEP, STEP), STEP)
+        stage[:, :, :, rows, :] = result.reshape(freq, chans, 2, STEP, cols).astype(jnp.bfloat16)
+        for d in range(1, freq):
+            handover(i, d).start()
+        own_part(i).start()
+        return carry
+
+    lax.fori_loop(0, steps, filter_step, 0)
+
+    def filter_wait(i, carry):
+        for d in range(1, freq):
+            handover(i, d).wait()
+        own_part(i).wait()
+        return carry
+
+    lax.fori_loop(0, steps, filter_wait, 0)
+
+    mine = pl.ds(pl.multiple_of(me * chunk, 8), chunk)
+
+    def tile_sum(at):
+        sends = []
+        for d in range(1, tile):
+            peer = lax.rem(me + d, tile)
+            copy = pltpu.make_async_remote_copy(
+                src_ref=part_ref.at[at, pl.ds(pl.multiple_of(peer * chunk, 8), chunk)],
+                dst_ref=land_ref.at[at, d - 1],
+                send_sem=r_send.at[at, d - 1],
+                recv_sem=r_recv.at[at, d - 1],
+                device_id={"tile": peer},
+                device_id_type=MESH,
+            )
+            copy.start()
+            sends.append(copy)
+        total = part_ref[at, mine]
+        for d in range(1, tile):
+            sends[d - 1].wait_recv()
+            total = total + land_ref[at, d - 1]
+        sum_ref[at, mine] = total
+        for d in range(1, tile):
+            copy = pltpu.make_async_remote_copy(
+                src_ref=sum_ref.at[at, mine],
+                dst_ref=sum_ref.at[at, mine],
+                send_sem=g_send.at[at, d - 1],
+                recv_sem=g_recv.at[at, d - 1],
+                device_id={"tile": lax.rem(me + d, tile)},
+                device_id_type=MESH,
+            )
+            copy.start()
+            sends.append(copy)
+        for copy in sends[tile - 1 :]:
+            copy.wait_recv()
+        return sends
+
+    def rows_of(c):
+        return slice(2 * k * c, 2 * k * (c + 1))
+
+    part_ref[...] = jnp.zeros_like(part_ref)
+    for c in range(chans):
+        part_ref[0, rows_of(c), :spectra] = project(start_ref[...], v_ref[c, 0], v_ref[c, 1], k)
+    pending = tile_sum(0)
+    for step_at in range(ITERS):
+        for c in range(chans):
+            weights = sum_ref[step_at, rows_of(c), :spectra]
+            if step_at == 0:
+                basis = start_ref[...]
+            else:
+                m_re, m_im = inverse_factor(sum_ref[step_at, rows_of(c), base:], k, off)
+                weights = mix(m_re, m_im, weights, k)
+                basis = mix(m_re, m_im, z_ref[c], k)
+            real_v, imag_v = v_ref[c, 0], v_ref[c, 1]
+            parts = split3(weights / spectra)
+            on_re = fold3(plain(parts, real_v))
+            on_im = fold3(plain(parts, imag_v))
+            z = jnp.concatenate([on_re[:k] - on_im[k:], on_re[k:] + on_im[:k]], axis=0) + loading * basis
+            z_ref[c] = z
+            before = [jnp.zeros((off, width), jnp.float32)] if off else []
+            after = jnp.zeros((128 - off - k, width), jnp.float32)
+            dims = (((1,), (1,)), ((), ()))
+            on_zr, on_zi = [
+                lax.dot_general(
+                    z, jnp.concatenate(before + [half, after], axis=0), dims,
+                    precision=highest, preferred_element_type=jnp.float32,
+                )
+                for half in (z[:k], z[k:])
+            ]
+            gram = jnp.concatenate([on_zr[:k] + on_zi[k:], on_zi[:k] - on_zr[k:]], axis=0)
+            part_ref[step_at + 1, rows_of(c), base:] = gram
+            part_ref[step_at + 1, rows_of(c), :spectra] = project(z, real_v, imag_v, k)
+        pending += tile_sum(step_at + 1)
+
+    n2 = 2 * k
+    stride = tile * cols
+
+    def give(c, d, f):
+        peer = lax.rem(me + d, tile)
+        lanes = pl.ds(pl.multiple_of(f * stride + me * cols, cols), cols)
+        src = give_ref.at[peer, :, c, :, f * cols : (f + 1) * cols]
+        dst = out_ref.at[:, c, :, lanes]
+        if d == 0:
+            return pltpu.make_async_copy(src, dst, own_sem.at[c * freq + f])
+        return pltpu.make_async_remote_copy(
+            src_ref=src,
+            dst_ref=dst,
+            send_sem=o_send.at[c, d - 1, f],
+            recv_sem=o_recv.at[c, d - 1, f],
+            device_id={"tile": peer},
+            device_id_type=MESH,
+        )
+
+    copies = []
+    for c in range(chans):
+        m_re, m_im = inverse_factor(sum_ref[ITERS, rows_of(c), base:], k, off)
+        w = mix(m_re, m_im, sum_ref[ITERS, rows_of(c), :spectra], k)
+        q = mix(m_re, m_im, z_ref[c], k)
+        turned = jnp.concatenate([q[k:], -q[:k]], axis=0)
+        w3 = split3(w)
+        w_left = jnp.concatenate([w3[:n2], w3[:n2], w3[n2 : 2 * n2], w3[n2 : 2 * n2], w3[:n2], w3[2 * n2 :]], axis=0)
+        for r, side in ((0, q), (1, turned)):
+            s3 = split3(side)
+            s_right = jnp.concatenate(
+                [s3[:n2], s3[n2 : 2 * n2], s3[:n2], s3[n2 : 2 * n2], s3[2 * n2 :], s3[:n2]], axis=0
+            )
+            cleaned = v_ref[c, r].astype(jnp.float32) - tn(w_left, s_right)
+            give_ref[:, r, c] = cleaned.reshape(tile, block, width).astype(jnp.bfloat16)
+        for d in range(tile):
+            for f in range(freq):
+                copy = give(c, d, f)
+                copy.start()
+                copies.append(copy)
+    for copy in copies:
+        copy.wait()
+    for copy in pending:
+        copy.wait_send()
+
+
+def channelize_kernel(volts_ref, table_ref, out_ref):
+    step = pl.program_id(0)
+    span = (STEP + TAPS - 1) * P_SIZE
+    start = pl.multiple_of(step * (STEP * P_SIZE), P_SIZE)
+    chunk = volts_ref[:, pl.ds(start, span)]
+    result = nt(table_ref[...], chunk)
+    out_ref[...] = result.reshape(out_ref.shape).astype(jnp.bfloat16)
+
+
+def channelize(voltages, table, rows, spectra_all):
+    inputs_local, samples = voltages.shape
+    return pl.pallas_call(
+        channelize_kernel,
+        grid=(spectra_all // STEP,),
+        in_specs=[VMEM, VMEM],
+        out_specs=pl.BlockSpec((rows, STEP, inputs_local), lambda i: (0, i, 0)),
+        out_shape=jax.ShapeDtypeStruct((rows, spectra_all, inputs_local), jnp.bfloat16),
+        compiler_params=pltpu.CompilerParams(vmem_limit_bytes=40 * 2**20),
+    )(voltages, table)
 
 
 def start_kernel(v_ref, q_ref, pg_ref, *, k, lanes):
@@ -166,10 +349,6 @@
 
 def lanes_pad(k):
     return 128 - k
-
-
-def tn(left, right):
-    return lax.dot_general(left, right, (((0,), (0,)), ((), ())), preferred_element_type=jnp.float32)
 
 
 def clean_kernel(v_ref, z_ref, pg_ref, out_ref, *, k, lanes):
@@ -257,7 +436,7 @@
     return -(-value // unit) * unit
 
 
-def body(voltages, channel_ids, start_basis):
+def body_split(voltages, channel_ids, start_basis):
     inputs_local, samples_count = voltages.shape
     freq_count = lax.axis_size("freq")
     tile_count = lax.axis_size("tile")
@@ -309,6 +488,62 @@
     return moved.reshape(2, chan_local, spectra_local, freq_count * tile_count * inputs_local)
 
 
+def body(voltages, channel_ids, start_basis):
+    inputs_local, samples_count = voltages.shape
+    freq_count = lax.axis_size("freq")
+    tile_count = lax.axis_size("tile")
+    if inputs_local % 128:
+        return body_split(voltages, channel_ids, start_basis)
+    channels = channel_ids.shape[0]
+    chan_local = channels // freq_count
+    spectra_all = samples_count // P_SIZE - TAPS + 1
+    spectra_local = spectra_all // tile_count
+    k = start_basis.shape[1]
+    width = freq_count * inputs_local
+
+    coeffs = make_table(channel_ids, TAPS, P_SIZE)
+    coeffs = coeffs.reshape(TAPS, 2, channels, P_SIZE).transpose(0, 2, 1, 3).reshape(TAPS, 2 * channels, P_SIZE)
+    mine = lax.axis_index("tile")
+    start = start_basis.reshape(2 * k, freq_count, tile_count, inputs_local)
+    start = lax.dynamic_index_in_dim(start, mine, 2, keepdims=False).reshape(2 * k, width)
+
+    base, off = spectra_all // 128 * 128, spectra_all % 128
+    if off + k > 128:
+        base, off = base + 128, 0
+    rows = tile_count * up(-(-chan_local * 2 * k // tile_count), 8)
+    chunk = rows // tile_count
+    rounds = ITERS + 1
+    peers = tile_count - 1
+    steps = spectra_all // STEP
+    sem = pltpu.SemaphoreType.DMA
+    cleaned = pl.pallas_call(
+        functools.partial(fused_kernel, k=k, freq=freq_count, tile=tile_count, base=base, off=off),
+        in_specs=[VMEM] * 3,
+        out_specs=VMEM,
+        out_shape=jax.ShapeDtypeStruct(
+            (2, chan_local, spectra_local, width * tile_count), jnp.bfloat16
+        ),
+        scratch_shapes=[
+            pltpu.VMEM((freq_count, chan_local, 2, spectra_all, inputs_local), jnp.bfloat16),
+            pltpu.VMEM((chan_local, 2, spectra_all, width), jnp.bfloat16),
+            pltpu.VMEM((chan_local, 2 * k, width), jnp.float32),
+            pltpu.VMEM((rounds, rows, base + 128), jnp.float32),
+            pltpu.VMEM((rounds, peers, chunk, base + 128), jnp.float32),
+            pltpu.VMEM((rounds, rows, base + 128), jnp.float32),
+            pltpu.VMEM((tile_count, 2, chan_local, spectra_local, width), jnp.bfloat16),
+            sem((steps, freq_count - 1)), sem((steps, freq_count - 1)),
+            sem((rounds, peers)), sem((rounds, peers)),
+            sem((rounds, peers)), sem((rounds, peers)),
+            sem((chan_local, peers, freq_count)), sem((chan_local, peers, freq_count)),
+            sem((max(steps, chan_local * freq_count),)),
+        ],
+        compiler_params=pltpu.CompilerParams(
+            collective_id=0, has_side_effects=True, vmem_limit_bytes=56 * 2**20
+        ),
+    )(voltages, banded(coeffs), start)
+    return cleaned.astype(jnp.float32)
+
+
 def solution(mesh):
     in_specs = (P(("freq", "tile"), None), P(), P())
     out_specs = P(None, "freq", "tile", None)

time: 138 us -> 102 us (0.74)
  blocking collectives: 32.4 us -> 0 us
  Pallas kernels: 66 us -> 93.6 us
  waiting for transfers between devices: 14.4 us -> 0 us
  local copies, waits for them, and re-layouts: 16.4 us -> 2.22 us
  starting transfers between devices: 4.26 us -> 0 us
  other arithmetic: 2.39 us -> 5.49 us
    all_to_all x1 -> x0, blocking collectives: 32.4 us -> none  [body(): lax.all_to_all(cleaned, 'tile', split_axis=0, concat_axis=0, tiled=True)]
    pallas_call x10 -> x1, Pallas kernels: 66 us -> 93.6 us  [body(): pl.pallas_call(functools.partial(fused_kernel, k=k, freq=freq_count, tile...]
    all_to_all x1 -> x0, waiting for transfers between devices: 14.4 us -> none  [body(): lax.all_to_all(parcel, 'freq', split_axis=1, concat_axis=1, tiled=True)]
    reshape x5 -> x0, local copies, waits for them, and re-layouts: 8.14 us -> none  [the longest x3 6.9 us: body(): moved.reshape(2, chan_local, spectra_local, freq_count * tile_count * inp...]
    unnamed x23 -> x5, local copies, waits for them, and re-layouts: 8.22 us -> 2.17 us
    all_to_all x1 -> x0, starting transfers between devices: 4.26 us -> none  [body(): lax.all_to_all(parcel, 'freq', split_axis=1, concat_axis=1, tiled=True)]
    convert_element_type x0 -> x1, other arithmetic: none -> 2.93 us  [body(): return cleaned.astype(jnp.float32)]
  transfers between devices with their start and end apart: 1 -> 0, of which waited for: 1 -> 0; matrix products, arithmetic and copies ran while one was open for 0% -> 0% of each run, Pallas kernels for 0% -> 0%
where the time goes in v1:
time: 102 us
  Pallas kernels  93.6 us (92%)
  other arithmetic  5.49 us (5%)
  local copies, waits for them, and re-layouts  2.22 us (2%)
    pallas_call x1, Pallas kernels, body(): pl.pallas_call(functools.partial(fused_kernel, k=k, freq=freq_count, tile...  93.6 us
    convert_element_type x1, other arithmetic, body(): return cleaned.astype(jnp.float32)  2.93 us
    unnamed x5, local copies, waits for them, and re-layouts  2.17 us

profile of v1, /device:TPU:1, one launch (start us, length us, event | category | flops | bytes accessed | tf_op | source)
XLA Modules:
  0.0 102.1 jit_solution(9264399535677831279)
XLA Ops:
  0.0 0.9 fusion.7
  1.0 0.7 fusion.41
  2.3 0.1 fusion.17
  2.4 0.9 select_select_fusion
  3.3 0.0 copy-start
  3.3 1.5 %copy.12 = bf16[48,8,19,128]{3,1,2,0:T(8,128)(2,1)} copy(bf16[48,8,19,128]{3,2,1,0:T(8,128)(2,1)S(1)} %bitcast.22) | data formatting | bytes 3735552
  4.8 0.0 copy-done
  4.8 0.1 copy.8
  4.9 0.6 copy.13
  5.5 93.6 %shard_map.37 = bf16[2,3,24,4096]{3,2,1,0:T(8,128)(2,1)} custom-call(bf16[128,24960]{1,0:T(8,128)(2,1)} %volts_ref.1, bf16[384,2432]{1,0:T(8,128)(2,1)} %bitcast.23, f32[16,512]{1,0:T(8,128)} %bitcast.26), custom_call_target="tpu_custom_call" | custom-call | tf_op jit(solution)/shard_map/pallas_call | solution.py:519
  99.2 2.9 %convert_element_type.28 = f32[2,3,24,4096]{3,2,1,0:T(8,128)} convert(bf16[2,3,24,4096]{3,2,1,0:T(8,128)(2,1)} %shard_map.37) | non-fusion elementwise | flops 589824 | bytes 3538944 | tf_op jit(solution)/shard_map/convert_element_type | solution.py:544
  (6 shorter events, 0.1 us)
Async XLA Ops:
  3.3 1.5 %copy-start = (f32[2,8,4096]{2,1,0:T(8,128)S(1)}, f32[2,8,4096]{2,1,0:T(8,128)}, u32[]{:S(2)}) copy-start(f32[2,8,4096]{2,1,0:T(8,128)} %param.5) | copy-start | bytes 786436

commit v2 on v1

--- a/solution.py
+++ b/solution.py
@@ -40,6 +40,16 @@
     for tap in range(TAPS):
         table = jnp.where(frame - spect == tap, coeffs[tap][:, None, None, :], table)
     return table.reshape(rows * STEP, (STEP + TAPS - 1) * P_SIZE)
+
+
+def banded_frames(coeffs):
+    rows = coeffs.shape[1]
+    shape = (STEP + TAPS - 1, 1, STEP, 1)
+    lag = lax.broadcasted_iota(jnp.int32, shape, 0) - lax.broadcasted_iota(jnp.int32, shape, 2)
+    table = jnp.zeros((STEP + TAPS - 1, rows, STEP, P_SIZE), jnp.bfloat16)
+    for tap in range(TAPS):
+        table = jnp.where(lag == tap, coeffs[tap][None, :, None, :], table)
+    return table.reshape(STEP + TAPS - 1, rows * STEP, P_SIZE)
 
 
 def nt(left, right):
@@ -114,7 +124,7 @@
 def fused_kernel(
     volts_ref, table_ref, start_ref, out_ref,
     stage, v_ref, z_ref, part_ref, land_ref, sum_ref, give_ref,
-    f_send, f_recv, r_send, r_recv, g_send, g_recv, o_send, o_recv, own_sem,
+    volts_vmem, volts_sem, f_send, f_recv, r_send, r_recv, g_send, g_recv, o_send, o_recv, own_sem,
     *, k, freq, tile, base, off,
 ):
     chans, _, spectra, width = v_ref.shape
@@ -129,7 +139,24 @@
         pl.semaphore_signal(barrier, inc=1, device_id={"freq": lax.rem(group + d, freq)}, device_id_type=MESH)
     for d in range(1, tile):
         pl.semaphore_signal(barrier, inc=1, device_id={"tile": lax.rem(me + d, tile)}, device_id_type=MESH)
+    lead = (TAPS - 1) * P_SIZE
+
+    def fetch(i):
+        at = pl.ds(pl.multiple_of(lead + i * (STEP * P_SIZE), P_SIZE), STEP * P_SIZE)
+        return pltpu.make_async_copy(volts_ref.at[:, at], volts_vmem.at[:, at], volts_sem.at[i])
+
+    head = pltpu.make_async_copy(
+        volts_ref.at[:, :lead], volts_vmem.at[:, :lead], volts_sem.at[steps]
+    )
+    head.start()
+
+    def fetch_start(i, carry):
+        fetch(i).start()
+        return carry
+
+    lax.fori_loop(0, steps, fetch_start, 0)
     pl.semaphore_wait(barrier, freq - 1 + tile - 1)
+    head.wait()
 
     span = (STEP + TAPS - 1) * P_SIZE
     my_cols = pl.ds(pl.multiple_of(group * cols, cols), cols)
@@ -154,7 +181,9 @@
 
     def filter_step(i, carry):
         start = pl.multiple_of(i * (STEP * P_SIZE), P_SIZE)
-        result = nt(table_ref[...], volts_ref[:, pl.ds(start, span)])
+        fetch(i).wait()
+        table = jnp.concatenate([table_ref[at] for at in range(STEP + TAPS - 1)], axis=1)
+        result = nt(table, volts_vmem[:, pl.ds(start, span)])
         rows = pl.ds(pl.multiple_of(i * STEP, STEP), STEP)
         stage[:, :, :, rows, :] = result.reshape(freq, chans, 2, STEP, cols).astype(jnp.bfloat16)
         for d in range(1, freq):
@@ -518,7 +547,7 @@
     sem = pltpu.SemaphoreType.DMA
     cleaned = pl.pallas_call(
         functools.partial(fused_kernel, k=k, freq=freq_count, tile=tile_count, base=base, off=off),
-        in_specs=[VMEM] * 3,
+        in_specs=[pl.BlockSpec(memory_space=pl.ANY), VMEM, VMEM],
         out_specs=VMEM,
         out_shape=jax.ShapeDtypeStruct(
             (2, chan_local, spectra_local, width * tile_count), jnp.bfloat16
@@ -531,6 +560,8 @@
             pltpu.VMEM((rounds, peers, chunk, base + 128), jnp.float32),
             pltpu.VMEM((rounds, rows, base + 128), jnp.float32),
             pltpu.VMEM((tile_count, 2, chan_local, spectra_local, width), jnp.bfloat16),
+            pltpu.VMEM((inputs_local, samples_count), jnp.bfloat16),
+            sem((steps + 1,)),
             sem((steps, freq_count - 1)), sem((steps, freq_count - 1)),
             sem((rounds, peers)), sem((rounds, peers)),
             sem((rounds, peers)), sem((rounds, peers)),
@@ -540,7 +571,7 @@
         compiler_params=pltpu.CompilerParams(
             collective_id=0, has_side_effects=True, vmem_limit_bytes=56 * 2**20
         ),
-    )(voltages, banded(coeffs), start)
+    )(voltages, banded_frames(coeffs), start)
     return cleaned.astype(jnp.float32)
 
 

time: 102 us -> 106 us (1.039)
  other arithmetic: 5.49 us -> 10.5 us
  Pallas kernels: 93.6 us -> 91.9 us
    select_n x1, other arithmetic: 0.87 us -> 5.87 us  [banded_frames(): table = jnp.where(lag == tap, coeffs[tap][None, :, None, :], table)]
    pallas_call x1, Pallas kernels: 93.6 us -> 91.9 us  [body(): pl.pallas_call(functools.partial(fused_kernel, k=k, freq=freq_count, tile...]
    unnamed x5 -> x2, local copies, waits for them, and re-layouts: 2.17 us -> 1.61 us
where the time goes in v2:
time: 106 us
  Pallas kernels  91.9 us (87%)
  other arithmetic  10.5 us (10%)
  local copies, waits for them, and re-layouts  2.42 us (2%)
    pallas_call x1, Pallas kernels, body(): pl.pallas_call(functools.partial(fused_kernel, k=k, freq=freq_count, tile...  91.9 us
    select_n x1, other arithmetic, banded_frames(): table = jnp.where(lag == tap, coeffs[tap][None, :, None, :], table)  5.87 us
    convert_element_type x1, other arithmetic, body(): return cleaned.astype(jnp.float32)  2.93 us

profile of v2, /device:TPU:1, one launch (start us, length us, event | category | flops | bytes accessed | tf_op | source)
XLA Modules:
  0.0 105.7 jit_solution(3967991225255952245)
XLA Ops:
  0.0 0.7 fusion.41
  1.4 0.1 fusion.17
  1.5 0.9 fusion.7
  2.5 0.2 broadcast_in_dim.119
  2.7 0.2 broadcast_in_dim.112
  2.9 0.2 broadcast_in_dim.105
  3.1 0.2 broadcast_in_dim.98
  3.3 1.0 copy.7
  4.4 0.6 copy.10
  5.0 5.9 %select_select_fusion.table_ref = bf16[19,384,128]{2,1,0:T(8,128)(2,1)} fusion(pred[19,384]{1,0:T(8,128)(4,1)S(1)} %broadcast_in_dim.119, pred[19,384]{1,0:T(8,128)(4,1)S(1)} %broadcast_in_dim.112, pred[19,384]{1,0:T(8,128)(4,1)S(1)} %broadcast_in_dim.105, pred[19,384]{1,0:T(8,128)(4,1)S(1)} %broadcast_in_dim.98, bf16[384,128]{1,0:T(8,128)(2,1)S(1)} %bitcast.21, ...), kind=kLoop, calls=%fused_computation | loop fusion | flops 3735552 | bytes 2290176 | tf_op jit(solution)/shard_map/jit(_where)/select_n | solution.py:51
  10.8 91.9 %shard_map.37 = bf16[2,3,24,4096]{3,2,1,0:T(8,128)(2,1)} custom-call(bf16[128,24960]{1,0:T(8,128)(2,1)} %volts_ref.1, bf16[19,384,128]{2,1,0:T(8,128)(2,1)} %select_select_fusion.table_ref, f32[16,512]{1,0:T(8,128)} %bitcast.27), custom_call_target="tpu_custom_call" | custom-call | tf_op jit(solution)/shard_map/pallas_call | solution.py:548
  102.8 2.9 %convert_element_type.28 = f32[2,3,24,4096]{3,2,1,0:T(8,128)} convert(bf16[2,3,24,4096]{3,2,1,0:T(8,128)(2,1)} %shard_map.37) | non-fusion elementwise | flops 589824 | bytes 3538944 | tf_op jit(solution)/shard_map/convert_element_type | solution.py:575
  (16 shorter events, 0.3 us)
